TPU v7x, 512 devices: a whole 4x4x16 slice. The times are simulated.
512 devices in a mesh: clus: 64 (over x, z_hi, y), samp: 8 (over z_lo, core).
Axes of the slice: x: 4, y: 4, z: 16 (z_hi: 4, z_lo: 4; z = z_hi * 4 + z_lo), core: 2. Of those that a mesh axis runs over, the one named last changes fastest.
Arguments:
- child_patterns: float32 [2048, 2, 24, 512], P('clus', None, 'samp'), may hold values from -6 to 6
- theta_weights: float32 [6, 9], replicated, may hold values from -0.4 to 0.6
- phi_stencil: int32 [1024, 6], replicated, may hold values from 0 to 511, as said below
- phi_weights: float32 [1024, 6], replicated, may hold values from -0.3 to 0.7
- shift_phase: float32 [8, 48, 1024], P(None, 'samp'), may hold values from -3.140625 to 3.140625
- translation_table: float32 [16, 2, 48, 1024], P(None, None, 'samp', 'clus'), may hold values from -1.25 to 1.25
- far_list: int32 [256, 12], replicated, may hold values from 0 to 255, as said below
- far_vector: int32 [256, 12], replicated, may hold values from 0 to 15
Outputs:
- parent_incoming: float32 [256, 2, 48, 1024], P('clus', None, 'samp')
- child_incoming: float32 [2048, 2, 24, 512], P('clus', None, 'samp')
Inputs may be any that keep to these rules, and one draw needn't show every extreme that they name: `far_list`: row i names 12 different parent clusters, never i itself. `phi_stencil`: row n names 6 cyclically consecutive child columns starting at n // 2 - 6 // 2 + 1 or one column later.
All inputs are finite; a program needn't handle non-finite values.
Results may differ from a plain program's by a relative error of at most 0.00007.
Values sent between devices are 32-bit elements; how exact they have to be, the bound alone decides.
A program may use at most 128 MiB of HBM per device.

v0:
```python
import jax
import jax.numpy as jnp
from jax import lax
from jax.sharding import PartitionSpec as P

P_SIZE = 6
HIGH = lax.Precision.HIGH


def shifted(value, axis, by):
    peers = lax.axis_size(axis)
    return lax.ppermute(value, axis, [(i, (i + by) % peers) for i in range(peers)])


def phi_table(phi_stencil, phi_weights, columns):
    positions = jnp.arange(columns, dtype=jnp.int32)
    total = jnp.zeros((columns, phi_stencil.shape[0]), jnp.float32)
    for point in range(phi_stencil.shape[1]):
        hits = (phi_stencil[None, :, point] == positions[:, None]).astype(jnp.float32)
        total = total + hits * phi_weights[None, :, point]
    return total


def per_device(
    child_patterns,
    theta_weights,
    phi_stencil,
    phi_weights,
    shift_phase,
    translation_table,
    far_list,
    far_vector,
):
    groups = child_patterns.shape[0] // 8
    columns = child_patterns.shape[3]
    rows_parent = theta_weights.shape[0]
    azimuth = phi_stencil.shape[0]
    margin = P_SIZE // 2
    below = shifted(child_patterns, "samp", 1)
    above = shifted(child_patterns, "samp", -1)
    phi_matrix = phi_table(phi_stencil, phi_weights, columns)
    cosine = jnp.cos(shift_phase)
    sine = jnp.sin(shift_phase)
    extended = jnp.concatenate([below, child_patterns, above], axis=2)
    tilted = jnp.stack(
        [
            sum((theta_weights[a, b] * extended[:, :, b] for b in range(9)))
            for a in range(rows_parent)
        ],
        axis=2,
    )
    refined = jnp.einsum("cqap,pn->cqan", tilted, phi_matrix, precision=HIGH)
    refined = refined.reshape(groups, 8, 2, rows_parent, azimuth)
    real_part = refined[:, :, 0] * cosine - refined[:, :, 1] * sine
    imag_part = refined[:, :, 0] * sine + refined[:, :, 1] * cosine
    outgoing = jnp.stack([jnp.sum(real_part, axis=1), jnp.sum(imag_part, axis=1)], axis=1)
    everyone = lax.all_to_all(outgoing, "clus", split_axis=3, concat_axis=0, tiled=True)
    clusters = everyone.shape[0]
    lanes = everyone.shape[2] * everyone.shape[3]
    flat = everyone.reshape(clusters, 2 * lanes)
    table = translation_table.reshape(translation_table.shape[0], 2 * lanes)
    pick = (far_list[:, :, None] == jnp.arange(clusters)[None, None, :]).astype(jnp.float32)
    pick_vec = (far_vector[:, :, None] == jnp.arange(table.shape[0])[None, None, :]).astype(
        jnp.float32
    )
    source = jnp.einsum("ilc,cs->lis", pick, flat, precision=HIGH)
    operator = jnp.einsum("ilv,vs->lis", pick_vec, table, precision=HIGH)
    s_re, s_im = (source[..., :lanes], source[..., lanes:])
    o_re, o_im = (operator[..., :lanes], operator[..., lanes:])
    in_re = jnp.sum(o_re * s_re - o_im * s_im, axis=0)
    in_im = jnp.sum(o_re * s_im + o_im * s_re, axis=0)
    landed = jnp.concatenate([in_re, in_im], axis=1).reshape(everyone.shape)
    incoming = lax.all_to_all(landed, "clus", split_axis=0, concat_axis=3, tiled=True)
    low_real = incoming[:, None, 0] * cosine + incoming[:, None, 1] * sine
    low_imag = incoming[:, None, 1] * cosine - incoming[:, None, 0] * sine
    lowered = jnp.stack([low_real, low_imag], axis=2).reshape(groups * 8, 2, rows_parent, azimuth)
    narrow = jnp.einsum("cqan,pn->cqap", lowered, phi_matrix, precision=HIGH)

    def back(first):
        return jnp.stack(
            [
                sum((theta_weights[a, b] * narrow[:, :, a] for a in range(rows_parent)))
                for b in range(first, first + margin)
            ],
            axis=2,
        )

    from_above = shifted(back(0), "samp", -1)
    from_below = shifted(back(2 * margin), "samp", 1)
    child_incoming = back(margin) + from_above + from_below
    return (incoming, child_incoming)


def solution(mesh):
    placed = (
        P("clus", None, "samp", None),
        P(),
        P(),
        P(),
        P(None, "samp", None),
        P(None, None, "samp", "clus"),
        P(),
        P(),
    )
    return jax.shard_map(
        per_device,
        mesh=mesh,
        in_specs=placed,
        out_specs=(P("clus", None, "samp", None), P("clus", None, "samp", None)),
        check_vma=False,
    )
```

profile of v0, /device:TPU:1, one launch (start us, length us, event | category | flops | bytes accessed | tf_op | source)
XLA Modules:
  0.0 206.6 jit_solution(3628376807708791519)
XLA Ops:
  0.6 1.1 copy.62
  1.7 4.9 %collective-permute-start = (f32[32,2,3,512]{3,0,2,1:T(8,128)S(1)}, f32[32,2,3,512]{3,0,2,1:T(8,128)S(1)}, u32[]{:S(2)}, u32[]{:S(2)}) collective-permute-start(f32[32,2,3,512]{3,0,2,1:T(8,128)S(1)} %copy.62), channel_id=1, source_target_pairs={{0,1},{1,2},{2,3},{3,4},{4,5},{5,6},{6,7},{7,0},{8,9},{9,10},{10,1... | collective-permute-start | bytes 1179656 | tf_op jit(solution)/shard_map/ppermute | solution.py:12
  6.6 5.7 %collective-permute-start.1 = (f32[32,2,3,512]{3,0,2,1:T(8,128)S(1)}, f32[32,2,3,512]{3,0,2,1:T(8,128)S(1)}, u32[]{:S(2)}, u32[]{:S(2)}) collective-permute-start(f32[32,2,3,512]{3,0,2,1:T(8,128)S(1)} %copy.62), channel_id=1, source_target_pairs={{0,7},{1,0},{2,1},{3,2},{4,3},{5,4},{6,5},{7,6},{8,15},{9,8},{10,9... | collective-permute-start | bytes 1179656 | tf_op jit(solution)/shard_map/ppermute | solution.py:12
  12.4 2.1 %fusion.24 = (f32[1,1]{1,0:T(1,128)}, f32[1,1]{1,0:T(1,128)}, f32[1,1]{1,0:T(1,128)}, f32[1,1]{1,0:T(1,128)}, f32[1,1]{1,0:T(1,128)}, /*index=5*/f32[1,1]{1,0:T(...) fusion(f32[6,9]{1,0:T(8,128)} %param.9), kind=kLoop, calls=%fused_computation.62 | loop fusion | bytes 152 | tf_op jit(solution)/shard_map/slice | solution.py:47
  14.5 1.0 fusion.21
  15.5 1.0 fusion.22
  16.5 2.0 fusion.25
  18.5 2.1 %fusion.23 = (f32[1,1]{1,0:T(1,128)}, f32[1,1]{1,0:T(1,128)}, f32[1,1]{1,0:T(1,128)}, f32[1,1]{1,0:T(1,128)}, f32[1,1]{1,0:T(1,128)}, /*index=5*/f32[1,1]{1,0:T(...) fusion(f32[6,9]{1,0:T(8,128)} %param.9), kind=kLoop, calls=%fused_computation.61 | loop fusion | bytes 152 | tf_op jit(solution)/shard_map/slice | solution.py:47
  20.6 1.6 fusion.20
  22.3 5.6 %add_dynamic-update-slice_fusion.5 = f32[32,2,6,512]{3,0,2,1:T(8,128)S(1)} fusion(f32[32,2,3,512]{3,0,2,1:T(8,128)S(1)} %collective-permute-done.1, f32[32,2,3,512]{3,0,2,1:T(8,128)S(1)} %copy.62, f32[32,2,3,512]{3,0,2,1:T(8,128)S(1)} %collective-permute-done, f32[]{:T(128)} %bitcast.9, f32[]{:T(128)} %bitcast.8, f32[]{:T(128)} %bitcast.7, f32[]{:T(128)} %bitcast.6, ...), kind=kLoop, calls=%fused_computation.50 | loop fusion | flops 557055 | bytes 1310756
  27.8 5.8 %add_dynamic-update-slice_fusion.4 = f32[32,2,6,512]{3,0,2,1:T(8,128)S(1)} fusion(f32[32,2,6,512]{3,0,2,1:T(8,128)S(1)} %add_dynamic-update-slice_fusion.5, f32[32,2,3,512]{3,0,2,1:T(8,128)S(1)} %collective-permute-done.1, f32[32,2,3,512]{3,0,2,1:T(8,128)S(1)} %copy.62, f32[32,2,3,512]{3,0,2,1:T(8,128)S(1)} %collective-permute-done, f32[]{:T(128)} %bitcast.18, ...), kind=kLoop, calls=%fused_computation.49 | loop fusion | flops 557056 | bytes 1310756
  33.7 6.0 %add_dynamic-update-slice_fusion.3 = f32[32,2,6,512]{3,0,2,1:T(8,128)S(1)} fusion(f32[32,2,6,512]{3,0,2,1:T(8,128)S(1)} %add_dynamic-update-slice_fusion.4, f32[32,2,3,512]{3,0,2,1:T(8,128)S(1)} %collective-permute-done.1, f32[32,2,3,512]{3,0,2,1:T(8,128)S(1)} %copy.62, f32[32,2,3,512]{3,0,2,1:T(8,128)S(1)} %collective-permute-done, f32[]{:T(128)} %bitcast.27, ...), kind=kLoop, calls=%fused_computation.48 | loop fusion | flops 557056 | bytes 1310756
  39.7 5.6 %add_dynamic-update-slice_fusion.2 = f32[32,2,6,512]{3,0,2,1:T(8,128)S(1)} fusion(f32[32,2,6,512]{3,0,2,1:T(8,128)S(1)} %add_dynamic-update-slice_fusion.3, f32[32,2,3,512]{3,0,2,1:T(8,128)S(1)} %collective-permute-done.1, f32[32,2,3,512]{3,0,2,1:T(8,128)S(1)} %copy.62, f32[32,2,3,512]{3,0,2,1:T(8,128)S(1)} %collective-permute-done, f32[]{:T(128)} %bitcast.36, ...), kind=kLoop, calls=%fused_computation.47 | loop fusion | flops 557056 | bytes 1310756
  45.3 5.8 %add_dynamic-update-slice_fusion.1 = f32[32,2,6,512]{3,0,2,1:T(8,128)S(1)} fusion(f32[32,2,6,512]{3,0,2,1:T(8,128)S(1)} %add_dynamic-update-slice_fusion.2, f32[32,2,3,512]{3,0,2,1:T(8,128)S(1)} %collective-permute-done.1, f32[32,2,3,512]{3,0,2,1:T(8,128)S(1)} %copy.62, f32[32,2,3,512]{3,0,2,1:T(8,128)S(1)} %collective-permute-done, f32[]{:T(128)} %bitcast.45, ...), kind=kLoop, calls=%fused_computation.46 | loop fusion | flops 557056 | bytes 1310756
  51.1 5.7 %add_dynamic-update-slice_fusion = f32[32,2,6,512]{3,0,2,1:T(8,128)S(1)} fusion(f32[32,2,6,512]{3,0,2,1:T(8,128)S(1)} %add_dynamic-update-slice_fusion.1, f32[32,2,3,512]{3,0,2,1:T(8,128)S(1)} %collective-permute-done.1, f32[32,2,3,512]{3,0,2,1:T(8,128)S(1)} %copy.62, f32[32,2,3,512]{3,0,2,1:T(8,128)S(1)} %collective-permute-done, f32[]{:T(128)} %bitcast.54, ...), kind=kLoop, calls=%fused_computation.45 | loop fusion | flops 557056 | bytes 1310756 | tf_op jit(solution)/shard_map/stack | solution.py:45
  56.8 2.8 %fusion.10 = f32[4,8,2,6,1024]{4,1,0,3,2:T(8,128)S(1)} fusion(f32[32,2,6,512]{3,0,2,1:T(8,128)S(1)} %add_dynamic-update-slice_fusion, f32[1024]{0:T(1024)S(1)} %bitcast.152, s32[1024]{0:T(1024)S(1)} %bitcast.140, f32[1024]{0:T(1024)S(1)} %bitcast.154, s32[1024]{0:T(1024)S(1)} %bitcast.142, f32[1024]{0:T(1024)S(1)} %bitcast.146, s32[1024]{0:T(1024)S(1)} %bitcast.134, ...), kind=kOutput, calls=%fused_computation.19 | convolution fusion | flops 1216872448 | bytes 2408448 | tf_op jit(solution)/shard_map/cqap,pn->cqan/dot_general | solution.py:52
  59.6 0.6 subtract_reduce_fusion.1
  60.3 3.2 %copy.67 = f32[4,2,6,1024]{2,0,1,3:T(4,128)} copy(f32[4,2,6,1024]{3,0,2,1:T(4,128)S(1)} %pad_maximum_fusion.2) | data formatting | bytes 393216 | tf_op jit(solution)/shard_map/stack | solution.py:56
  63.5 6.6 %reshape.140 = f32[64,1,768]{2,1,0:T(1,128)} reshape(f32[1024,2,4,6]{3,2,1,0:T(4,128)} %bitcast.123) | data formatting | bytes 393216
  70.1 16.5 %all-to-all-start = ((f32[64,1,768]{2,1,0:T(1,128)}), f32[64,1,768]{2,1,0:T(1,128)S(1)}, u32[]{:S(2)}, u32[]{:S(2)}) async-start(f32[64,1,768]{2,1,0:T(1,128)} %reshape.140), calls=%async_computation | async-start | bytes 393216 | tf_op jit(solution)/shard_map/all_to_all | solution.py:57
  86.7 0.8 convolution_bitcast_fusion
  87.5 19.5 %all-to-all-done = f32[64,1,768]{2,1,0:T(1,128)S(1)} async-done(((f32[64,1,768]{2,1,0:T(1,128)}), f32[64,1,768]{2,1,0:T(1,128)S(1)}, u32[]{:S(2)}, u32[]{:S(2)}) %all-to-all-start) | async-done | bytes 196640 | tf_op jit(solution)/shard_map/all_to_all | solution.py:57
  107.0 0.5 broadcast.152
  107.5 1.1 reduce
  108.6 6.8 %reshape.141 = f32[1024,2,4,6]{3,2,1,0:T(4,128)} reshape(f32[64,768]{1,0:T(8,128)S(1)} %reduce) | data formatting | bytes 393216
  115.4 6.0 %copy.80 = f32[4,2,6,64,16]{4,2,1,0,3:T(8,128)} copy(f32[4,2,6,64,16]{2,0,1,4,3:T(4,128)} %bitcast.124) | data formatting | bytes 393216 | tf_op jit(solution)/shard_map/all_to_all | solution.py:57
  121.4 2.4 %reshape.134 = f32[256,192]{1,0:T(8,128)S(1)} reshape(f32[64,4,2,6,16]{4,3,2,1,0:T(8,128)} %bitcast.125) | data formatting | bytes 393216 | tf_op jit(solution)/shard_map/reshape | solution.py:60
  123.8 2.9 %fusion.5 = f32[12,256,192]{1,2,0:T(8,128)S(1)} fusion(s32[256,12]{0,1:T(8,128)S(1)} %copy-done.3, f32[256,192]{1,0:T(8,128)S(1)} %reshape.134), kind=kOutput, calls=%fused_computation.14 | convolution fusion | flops 906756096 | bytes 2568192 | tf_op jit(solution)/shard_map/ilc,cs->lis/dot_general | solution.py:66
  126.7 0.5 subtract_reduce_fusion
  127.3 1.0 copy.71
  128.3 2.1 %reshape.142 = f32[64,1,768]{2,1,0:T(1,128)S(1)} reshape(f32[256,6,2,16]{3,2,1,0:T(2,128)S(1)} %bitcast.126) | data formatting | bytes 393216
  130.4 24.6 %all_to_all.33 = f32[64,1,768]{2,1,0:T(1,128)S(1)} all-to-all(f32[64,1,768]{2,1,0:T(1,128)S(1)} %reshape.142), channel_id=1, replica_groups=mesh['clus'=64,'samp'=8] {'clus'}, dimensions={0} | all-to-all | bytes 393216 | tf_op jit(solution)/shard_map/all_to_all | solution.py:73
  155.1 1.1 reduce.1
  156.2 2.1 %reshape.143 = f32[256,6,2,16]{3,2,1,0:T(2,128)S(1)} reshape(f32[64,768]{1,0:T(8,128)S(1)} %reduce.1) | data formatting | bytes 393216
  158.6 0.8 all_to_all.30
  159.9 2.8 %fusion.1 = f32[32,2,6,512]{3,0,2,1:T(8,128)S(1)} fusion(f32[32,1,6,1024]{3,0,2,1:T(8,128)S(1)} %get-tuple-element.17, f32[32,1,6,1024]{3,0,2,1:T(8,128)S(1)} %get-tuple-element.16, f32[1024]{0:T(1024)S(1)} %bitcast.153, s32[1024]{0:T(1024)S(1)} %bitcast.141, f32[1024]{0:T(1024)S(1)} %bitcast.155, s32[1024]{0:T(1024)S(1)} %bitcast.143, ...), kind=kOutput, calls=%fused_computation.2 | convolution fusion | flops 1217265664 | bytes 2408448 | tf_op jit(solution)/shard_map/cqan,pn->cqap/dot_general | solution.py:77
  162.8 3.9 %multiply_add_fusion.3 = f32[32,2,1,512]{3,0,2,1:T(8,128)S(1)} fusion(f32[32,2,6,512]{3,0,2,1:T(8,128)S(1)} %fusion.1, f32[]{:T(128)} %bitcast.48, f32[]{:T(128)} %bitcast.39, f32[]{:T(128)} %bitcast.30, f32[]{:T(128)} %bitcast.21, f32[]{:T(128)} %bitcast.12, f32[]{:T(128)} %bitcast.3), kind=kLoop, calls=%fused_computation.39 | loop fusion | flops 360448 | bytes 917528 | tf_op jit(solution)/shard_map/add | solution.py:82
  166.7 3.9 %multiply_add_fusion.4 = f32[32,2,1,512]{3,0,2,1:T(8,128)S(1)} fusion(f32[32,2,6,512]{3,0,2,1:T(8,128)S(1)} %fusion.1, f32[]{:T(128)} %bitcast.47, f32[]{:T(128)} %bitcast.38, f32[]{:T(128)} %bitcast.29, f32[]{:T(128)} %bitcast.20, f32[]{:T(128)} %bitcast.11, f32[]{:T(128)} %bitcast.2), kind=kLoop, calls=%fused_computation.40 | loop fusion | flops 360448 | bytes 917528 | tf_op jit(solution)/shard_map/add | solution.py:82
  170.6 4.1 %multiply_add_fusion.5 = f32[32,2,1,512]{3,0,2,1:T(8,128)S(1)} fusion(f32[32,2,6,512]{3,0,2,1:T(8,128)S(1)} %fusion.1, f32[]{:T(128)} %bitcast.46, f32[]{:T(128)} %bitcast.37, f32[]{:T(128)} %bitcast.28, f32[]{:T(128)} %bitcast.19, f32[]{:T(128)} %bitcast.10, f32[]{:T(128)} %bitcast.1), kind=kLoop, calls=%fused_computation.41 | loop fusion | flops 360448 | bytes 917528 | tf_op jit(solution)/shard_map/add | solution.py:82
  174.7 3.6 %multiply_add_fusion.1 = f32[32,2,1,512]{3,0,2,1:T(8,128)S(1)} fusion(f32[32,2,6,512]{3,0,2,1:T(8,128)S(1)} %fusion.1, f32[]{:T(128)} %bitcast.53, f32[]{:T(128)} %bitcast.44, f32[]{:T(128)} %bitcast.35, f32[]{:T(128)} %bitcast.26, f32[]{:T(128)} %bitcast.17, f32[]{:T(128)} %bitcast.8), kind=kLoop, calls=%fused_computation.37 | loop fusion | flops 360448 | bytes 917528 | tf_op jit(solution)/shard_map/add | solution.py:82
  178.4 3.7 %multiply_add_fusion.2 = f32[32,2,1,512]{3,0,2,1:T(8,128)S(1)} fusion(f32[32,2,6,512]{3,0,2,1:T(8,128)S(1)} %fusion.1, f32[]{:T(128)} %bitcast.52, f32[]{:T(128)} %bitcast.43, f32[]{:T(128)} %bitcast.34, f32[]{:T(128)} %bitcast.25, f32[]{:T(128)} %bitcast.16, f32[]{:T(128)} %bitcast.7), kind=kLoop, calls=%fused_computation.38 | loop fusion | flops 360448 | bytes 917528 | tf_op jit(solution)/shard_map/add | solution.py:82
  182.1 3.8 %multiply_add_fusion = f32[32,2,1,512]{3,0,2,1:T(8,128)S(1)} fusion(f32[32,2,6,512]{3,0,2,1:T(8,128)S(1)} %fusion.1, f32[]{:T(128)} %bitcast.54, f32[]{:T(128)} %bitcast.45, f32[]{:T(128)} %bitcast.36, f32[]{:T(128)} %bitcast.27, f32[]{:T(128)} %bitcast.18, f32[]{:T(128)} %bitcast.9), kind=kLoop, calls=%fused_computation.36 | loop fusion | flops 360448 | bytes 917528 | tf_op jit(solution)/shard_map/add | solution.py:82
  185.9 3.6 %multiply_add_fusion.6 = f32[32,2,1,512]{3,0,2,1:T(8,128)S(1)} fusion(f32[32,2,6,512]{3,0,2,1:T(8,128)S(1)} %fusion.1, f32[]{:T(128)} %bitcast.51, f32[]{:T(128)} %bitcast.42, f32[]{:T(128)} %bitcast.33, f32[]{:T(128)} %bitcast.24, f32[]{:T(128)} %bitcast.15, f32[]{:T(128)} %bitcast.6), kind=kLoop, calls=%fused_computation.42 | loop fusion | flops 360448 | bytes 917528 | tf_op jit(solution)/shard_map/add | solution.py:82
  189.6 5.3 %collective-permute-start.2 = (f32[32,2,3,512]{3,0,2,1:T(8,128)S(1)}, f32[32,2,3,512]{3,0,2,1:T(8,128)S(1)}, u32[]{:S(2)}, u32[]{:S(2)}) collective-permute-start(f32[32,2,3,512]{3,0,2,1:T(8,128)S(1)} %pad_maximum_fusion), channel_id=1, source_target_pairs={{0,7},{1,0},{2,1},{3,2},{4,3},{5,4},{6,5},{7,6},{8,15},{9,8},{10,9... | collective-permute-start | bytes 1179656 | tf_op jit(solution)/shard_map/ppermute | solution.py:12
  194.9 2.8 %collective-permute-start.3 = (f32[32,2,3,512]{3,0,2,1:T(8,128)S(1)}, f32[32,2,3,512]{3,0,2,1:T(8,128)S(1)}, u32[]{:S(2)}, u32[]{:S(2)}) collective-permute-start(f32[32,2,3,512]{3,0,2,1:T(8,128)S(1)} %pad_maximum_fusion.1), channel_id=1, source_target_pairs={{0,1},{1,2},{2,3},{3,4},{4,5},{5,6},{6,7},{7,0},{8,9},{9,10},{10,1... | collective-permute-start | bytes 1179656 | tf_op jit(solution)/shard_map/ppermute | solution.py:12
  197.7 3.8 %multiply_add_fusion.7 = f32[32,2,1,512]{3,0,2,1:T(8,128)S(1)} fusion(f32[32,2,6,512]{3,0,2,1:T(8,128)S(1)} %fusion.1, f32[]{:T(128)} %bitcast.50, f32[]{:T(128)} %bitcast.41, f32[]{:T(128)} %bitcast.32, f32[]{:T(128)} %bitcast.23, f32[]{:T(128)} %bitcast.14, f32[]{:T(128)} %bitcast.5), kind=kLoop, calls=%fused_computation.43 | loop fusion | flops 360448 | bytes 917528 | tf_op jit(solution)/shard_map/add | solution.py:82
  201.5 3.9 %multiply_add_fusion.8 = f32[32,2,1,512]{3,0,2,1:T(8,128)S(1)} fusion(f32[32,2,6,512]{3,0,2,1:T(8,128)S(1)} %fusion.1, f32[]{:T(128)} %bitcast.49, f32[]{:T(128)} %bitcast.40, f32[]{:T(128)} %bitcast.31, f32[]{:T(128)} %bitcast.22, f32[]{:T(128)} %bitcast.13, f32[]{:T(128)} %bitcast.4), kind=kLoop, calls=%fused_computation.44 | loop fusion | flops 360448 | bytes 917528 | tf_op jit(solution)/shard_map/add | solution.py:82
  205.6 1.1 copy.76
  (24 shorter events, 1.1 us)
Async XLA Ops:
  1.7 20.5 %collective-permute-start = (f32[32,2,3,512]{3,0,2,1:T(8,128)S(1)}, f32[32,2,3,512]{3,0,2,1:T(8,128)S(1)}, u32[]{:S(2)}, u32[]{:S(2)}) collective-permute-start(f32[32,2,3,512]{3,0,2,1:T(8,128)S(1)} %copy.62), channel_id=1, source_target_pairs={{0,1},{1,2},{2,3},{3,4},{4,5},{5,6},{6,7},{7,0},{8,9},{9,10},{10,1... | collective-permute-start | bytes 1179656 | tf_op jit(solution)/shard_map/ppermute | solution.py:12
  6.6 15.6 %collective-permute-start.1 = (f32[32,2,3,512]{3,0,2,1:T(8,128)S(1)}, f32[32,2,3,512]{3,0,2,1:T(8,128)S(1)}, u32[]{:S(2)}, u32[]{:S(2)}) collective-permute-start(f32[32,2,3,512]{3,0,2,1:T(8,128)S(1)} %copy.62), channel_id=1, source_target_pairs={{0,7},{1,0},{2,1},{3,2},{4,3},{5,4},{6,5},{7,6},{8,15},{9,8},{10,9... | collective-permute-start | bytes 1179656 | tf_op jit(solution)/shard_map/ppermute | solution.py:12
  63.5 23.1 %copy-start.1 = (f32[16,2,6,16]{3,1,2,0:T(2,128)S(1)}, f32[16,2,6,16]{3,1,2,0:T(2,128)}, u32[]{:S(2)}) copy-start(f32[16,2,6,16]{3,1,2,0:T(2,128)} %param.13) | copy-start | bytes 36868
  63.5 23.2 %copy-start.2 = (s32[256,12]{0,1:T(8,128)S(1)}, s32[256,12]{0,1:T(8,128)}, u32[]{:S(2)}) copy-start(s32[256,12]{0,1:T(8,128)} %param.15) | copy-start | bytes 36868
  70.1 36.9 %all-to-all-start = ((f32[64,1,768]{2,1,0:T(1,128)}), f32[64,1,768]{2,1,0:T(1,128)S(1)}, u32[]{:S(2)}, u32[]{:S(2)}) async-start(f32[64,1,768]{2,1,0:T(1,128)} %reshape.140), calls=%async_computation | async-start | bytes 393216 | tf_op jit(solution)/shard_map/all_to_all | solution.py:57
  121.4 2.4 %copy-start.3 = (s32[256,12]{0,1:T(8,128)S(1)}, s32[256,12]{0,1:T(8,128)}, u32[]{:S(2)}) copy-start(s32[256,12]{0,1:T(8,128)} %param.14) | copy-start | bytes 36868
  159.4 3.3 %copy-start = (f32[4,2,6,1024]{3,1,2,0:T(2,128)}, f32[4,2,6,1024]{3,1,2,0:T(2,128)S(1)}, u32[]{:S(2)}) copy-start(f32[4,2,6,1024]{3,1,2,0:T(2,128)S(1)} %all_to_all.30) | copy-start | bytes 589828
  189.6 15.9 %collective-permute-start.2 = (f32[32,2,3,512]{3,0,2,1:T(8,128)S(1)}, f32[32,2,3,512]{3,0,2,1:T(8,128)S(1)}, u32[]{:S(2)}, u32[]{:S(2)}) collective-permute-start(f32[32,2,3,512]{3,0,2,1:T(8,128)S(1)} %pad_maximum_fusion), channel_id=1, source_target_pairs={{0,7},{1,0},{2,1},{3,2},{4,3},{5,4},{6,5},{7,6},{8,15},{9,8},{10,9... | collective-permute-start | bytes 1179656 | tf_op jit(solution)/shard_map/ppermute | solution.py:12
  194.9 10.6 %collective-permute-start.3 = (f32[32,2,3,512]{3,0,2,1:T(8,128)S(1)}, f32[32,2,3,512]{3,0,2,1:T(8,128)S(1)}, u32[]{:S(2)}, u32[]{:S(2)}) collective-permute-start(f32[32,2,3,512]{3,0,2,1:T(8,128)S(1)} %pad_maximum_fusion.1), channel_id=1, source_target_pairs={{0,1},{1,2},{2,3},{3,4},{4,5},{5,6},{6,7},{7,0},{8,9},{9,10},{10,1... | collective-permute-start | bytes 1179656 | tf_op jit(solution)/shard_map/ppermute | solution.py:12
where the time goes:
time: 208 us; the launch traced here: 207 us
  other arithmetic  72.8 us (35%)
  local copies, waits for them, and re-layouts  44.1 us (21%)
  starting transfers between devices  35.2 us (17%)
  blocking collectives  24.6 us (12%)
  waiting for transfers between devices  19.5 us (9%)
  matrix products  9.36 us (4%)
    add x9, other arithmetic, back(): sum((theta_weights[a, b] * narrow[:, :, a] for a in range(rows_parent)))  34.5 us
    unnamed x5, other arithmetic  28.8 us
    all_to_all x1, blocking collectives, per_device(): lax.all_to_all(landed, 'clus', split_axis=0, concat_axis=3, tiled=True)  24.6 us
    unnamed x15, local copies, waits for them, and re-layouts  19.8 us
    all_to_all x1, waiting for transfers between devices, per_device(): lax.all_to_all(outgoing, 'clus', split_axis=3, concat_axis=0, tiled=True)  19.5 us
    ppermute x4, starting transfers between devices, shifted(): lax.ppermute(value, axis, [(i, (i + by) % peers) for i in range(peers)])  18.8 us
    all_to_all x1, starting transfers between devices, per_device(): lax.all_to_all(outgoing, 'clus', split_axis=3, concat_axis=0, tiled=True)  16.5 us
    all_to_all x2, local copies, waits for them, and re-layouts, per_device(): lax.all_to_all(outgoing, 'clus', split_axis=3, concat_axis=0, tiled=True)  6.5 us
  transfers between devices with their start and end apart: 5, of which 1 were waited for; matrix products, arithmetic and copies ran while one was open for 9% of the time, Pallas kernels for 0%

commit v1 on v0

--- a/solution.py
+++ b/solution.py
@@ -5,6 +5,12 @@
 
 P_SIZE = 6
 HIGH = lax.Precision.HIGH
+
+
+def trade_parts(array, name, split, join):
+    cells = jnp.split(array, lax.axis_size(name), axis=split)
+    received = lax.all_to_all(jnp.stack(cells), name, 0, 0)
+    return jnp.concatenate(received, axis=join)
 
 
 def shifted(value, axis, by):
@@ -54,7 +60,7 @@
     real_part = refined[:, :, 0] * cosine - refined[:, :, 1] * sine
     imag_part = refined[:, :, 0] * sine + refined[:, :, 1] * cosine
     outgoing = jnp.stack([jnp.sum(real_part, axis=1), jnp.sum(imag_part, axis=1)], axis=1)
-    everyone = lax.all_to_all(outgoing, "clus", split_axis=3, concat_axis=0, tiled=True)
+    everyone = trade_parts(outgoing, "clus", 3, 0)
     clusters = everyone.shape[0]
     lanes = everyone.shape[2] * everyone.shape[3]
     flat = everyone.reshape(clusters, 2 * lanes)

time: 208 us -> 201 us (0.966)
  local copies, waits for them, and re-layouts: 44.1 us -> 29 us
  other arithmetic: 72.8 us -> 77.8 us
  blocking collectives: 24.6 us -> 27.8 us
  waiting for transfers between devices: 19.5 us -> 16.3 us
    unnamed x15 -> x55, local copies, waits for them, and re-layouts: 19.8 us -> 10.7 us
    unnamed x5 -> x68, other arithmetic: 28.8 us -> 33.5 us
    all_to_all x1, waiting for transfers between devices: 19.5 us -> 16.3 us  [trade_parts(): received = lax.all_to_all(jnp.stack(cells), name, 0, 0)]
    all_to_all x1, blocking collectives: 24.6 us -> 27.8 us  [per_device(): lax.all_to_all(landed, 'clus', split_axis=0, concat_axis=3, tiled=True)]
    all_to_all x2, local copies, waits for them, and re-layouts: 6.5 us -> 3.61 us  [trade_parts(): received = lax.all_to_all(jnp.stack(cells), name, 0, 0)]
    reshape x1 -> x0, local copies, waits for them, and re-layouts: 2.35 us -> none  [per_device(): flat = everyone.reshape(clusters, 2 * lanes)]
where the time goes in v1:
time: 201 us; the launch traced here: 199 us
  other arithmetic  77.8 us (39%)
  starting transfers between devices  37.2 us (19%)
  local copies, waits for them, and re-layouts  29 us (14%)
  blocking collectives  27.8 us (14%)
  waiting for transfers between devices  16.3 us (8%)
  matrix products  9.36 us (5%)
    add x9, other arithmetic, back(): sum((theta_weights[a, b] * narrow[:, :, a] for a in range(rows_parent)))  34.4 us
    unnamed x68, other arithmetic  33.5 us
    all_to_all x1, blocking collectives, per_device(): lax.all_to_all(landed, 'clus', split_axis=0, concat_axis=3, tiled=True)  27.8 us
    ppermute x4, starting transfers between devices, shifted(): lax.ppermute(value, axis, [(i, (i + by) % peers) for i in range(peers)])  20.4 us
    all_to_all x1, starting transfers between devices, trade_parts(): received = lax.all_to_all(jnp.stack(cells), name, 0, 0)  16.8 us
    all_to_all x1, waiting for transfers between devices, trade_parts(): received = lax.all_to_all(jnp.stack(cells), name, 0, 0)  16.3 us
    unnamed x55, local copies, waits for them, and re-layouts  10.7 us
    slice x3, local copies, waits for them, and re-layouts, per_device(): theta_weights[a, b] * extended[:, :, b]  6.21 us
  transfers between devices with their start and end apart: 5, of which 1 were waited for; matrix products, arithmetic and copies ran while one was open for 9% of the time, Pallas kernels for 0%

profile of v1, /device:TPU:1, one launch (start us, length us, event | category | flops | bytes accessed | tf_op | source)
XLA Modules:
  0.0 199.0 jit_solution(11224442211184242567)
XLA Ops:
  0.6 1.1 copy.252
  1.7 8.7 %collective-permute-start.1 = (f32[32,2,3,512]{3,0,2,1:T(8,128)S(1)}, f32[32,2,3,512]{3,0,2,1:T(8,128)S(1)}, u32[]{:S(2)}, u32[]{:S(2)}) collective-permute-start(f32[32,2,3,512]{3,0,2,1:T(8,128)S(1)} %copy.252), channel_id=1, source_target_pairs={{0,7},{1,0},{2,1},{3,2},{4,3},{5,4},{6,5},{7,6},{8,15},{9,8},{10,9... | collective-permute-start | bytes 1179656 | tf_op jit(solution)/shard_map/ppermute | solution.py:18
  10.5 1.9 collective-permute-start
  12.4 2.1 %fusion.88 = (f32[1,1]{1,0:T(1,128)}, f32[1,1]{1,0:T(1,128)}, f32[1,1]{1,0:T(1,128)}, f32[1,1]{1,0:T(1,128)}, f32[1,1]{1,0:T(1,128)}, /*index=5*/f32[1,1]{1,0:T(...) fusion(f32[6,9]{1,0:T(8,128)} %param.9), kind=kLoop, calls=%fused_computation.316 | loop fusion | bytes 152 | tf_op jit(solution)/shard_map/slice | solution.py:53
  14.5 1.0 fusion.85
  15.5 1.0 fusion.86
  16.6 2.0 %fusion.89 = (f32[1,1]{1,0:T(1,128)}, f32[1,1]{1,0:T(1,128)}, f32[1,1]{1,0:T(1,128)}, f32[1,1]{1,0:T(1,128)}, f32[1,1]{1,0:T(1,128)}, /*index=5*/f32[1,1]{1,0:T(...) fusion(f32[6,9]{1,0:T(8,128)} %param.9), kind=kLoop, calls=%fused_computation.317 | loop fusion | bytes 128 | tf_op jit(solution)/shard_map/slice | solution.py:53
  18.6 2.1 %fusion.87 = (f32[1,1]{1,0:T(1,128)}, f32[1,1]{1,0:T(1,128)}, f32[1,1]{1,0:T(1,128)}, f32[1,1]{1,0:T(1,128)}, f32[1,1]{1,0:T(1,128)}, /*index=5*/f32[1,1]{1,0:T(...) fusion(f32[6,9]{1,0:T(8,128)} %param.9), kind=kLoop, calls=%fused_computation.315 | loop fusion | bytes 152 | tf_op jit(solution)/shard_map/slice | solution.py:53
  20.7 1.6 fusion.84
  22.4 5.8 %constant_dynamic-update-slice_fusion.5 = f32[32,2,6,512]{3,0,2,1:T(8,128)S(1)} fusion(f32[32,2,3,512]{3,0,2,1:T(8,128)S(1)} %collective-permute-done.1, f32[32,2,3,512]{3,0,2,1:T(8,128)S(1)} %copy.252, f32[32,2,3,512]{3,0,2,1:T(8,128)S(1)} %collective-permute-done, f32[]{:T(128)} %bitcast.9, f32[]{:T(128)} %bitcast.8, f32[]{:T(128)} %bitcast.7, ...), kind=kLoop, calls=%fused_computation.166 | loop fusion | flops 557055 | bytes 1310756
  28.1 5.7 %constant_dynamic-update-slice_fusion.4 = f32[32,2,6,512]{3,0,2,1:T(8,128)S(1)} fusion(f32[32,2,6,512]{3,0,2,1:T(8,128)S(1)} %constant_dynamic-update-slice_fusion.5, f32[32,2,3,512]{3,0,2,1:T(8,128)S(1)} %collective-permute-done.1, f32[32,2,3,512]{3,0,2,1:T(8,128)S(1)} %copy.252, f32[32,2,3,512]{3,0,2,1:T(8,128)S(1)} %collective-permute-done, f32[]{:T(128)} %bitcast.18, ...), kind=kLoop, calls=%fused_computation.165 | loop fusion | flops 557056 | bytes 1310756
  33.8 5.7 %constant_dynamic-update-slice_fusion.3 = f32[32,2,6,512]{3,0,2,1:T(8,128)S(1)} fusion(f32[32,2,6,512]{3,0,2,1:T(8,128)S(1)} %constant_dynamic-update-slice_fusion.4, f32[32,2,3,512]{3,0,2,1:T(8,128)S(1)} %collective-permute-done.1, f32[32,2,3,512]{3,0,2,1:T(8,128)S(1)} %copy.252, f32[32,2,3,512]{3,0,2,1:T(8,128)S(1)} %collective-permute-done, f32[]{:T(128)} %bitcast.27, ...), kind=kLoop, calls=%fused_computation.164 | loop fusion | flops 557056 | bytes 1310756
  39.5 5.8 %constant_dynamic-update-slice_fusion.2 = f32[32,2,6,512]{3,0,2,1:T(8,128)S(1)} fusion(f32[32,2,6,512]{3,0,2,1:T(8,128)S(1)} %constant_dynamic-update-slice_fusion.3, f32[32,2,3,512]{3,0,2,1:T(8,128)S(1)} %collective-permute-done.1, f32[32,2,3,512]{3,0,2,1:T(8,128)S(1)} %copy.252, f32[32,2,3,512]{3,0,2,1:T(8,128)S(1)} %collective-permute-done, f32[]{:T(128)} %bitcast.36, ...), kind=kLoop, calls=%fused_computation.163 | loop fusion | flops 557056 | bytes 1310756
  45.3 5.6 %constant_dynamic-update-slice_fusion.1 = f32[32,2,6,512]{3,0,2,1:T(8,128)S(1)} fusion(f32[32,2,6,512]{3,0,2,1:T(8,128)S(1)} %constant_dynamic-update-slice_fusion.2, f32[32,2,3,512]{3,0,2,1:T(8,128)S(1)} %collective-permute-done.1, f32[32,2,3,512]{3,0,2,1:T(8,128)S(1)} %copy.252, f32[32,2,3,512]{3,0,2,1:T(8,128)S(1)} %collective-permute-done, f32[]{:T(128)} %bitcast.45, ...), kind=kLoop, calls=%fused_computation.162 | loop fusion | flops 557056 | bytes 1310756
  50.9 6.0 %constant_dynamic-update-slice_fusion = f32[32,2,6,512]{3,0,2,1:T(8,128)S(1)} fusion(f32[32,2,6,512]{3,0,2,1:T(8,128)S(1)} %constant_dynamic-update-slice_fusion.1, f32[32,2,3,512]{3,0,2,1:T(8,128)S(1)} %collective-permute-done.1, f32[32,2,3,512]{3,0,2,1:T(8,128)S(1)} %copy.252, f32[32,2,3,512]{3,0,2,1:T(8,128)S(1)} %collective-permute-done, f32[]{:T(128)} %bitcast.54, ...), kind=kLoop, calls=%fused_computation.161 | loop fusion | flops 557056 | bytes 1310756 | tf_op jit(solution)/shard_map/stack | solution.py:51
  57.0 2.8 %fusion.10 = f32[4,8,2,6,1024]{4,1,0,3,2:T(8,128)S(1)} fusion(f32[32,2,6,512]{3,0,2,1:T(8,128)S(1)} %constant_dynamic-update-slice_fusion, f32[1024]{0:T(1024)S(1)} %bitcast.404, s32[1024]{0:T(1024)S(1)} %bitcast.392, f32[1024]{0:T(1024)S(1)} %bitcast.406, s32[1024]{0:T(1024)S(1)} %bitcast.394, f32[1024]{0:T(1024)S(1)} %bitcast.398, ...), kind=kOutput, calls=%fused_computation.145 | convolution fusion | flops 1216872448 | bytes 2408448 | tf_op jit(solution)/shard_map/cqap,pn->cqan/dot_general | solution.py:58
  59.8 0.6 subtract_reduce_fusion.1
  65.9 1.9 reshape.135
  67.7 16.8 %all-to-all-start = ((f32[64,1,768]{2,1,0:T(1,128)}), f32[64,1,768]{2,1,0:T(1,128)S(1)}, u32[]{:S(2)}, u32[]{:S(2)}) async-start(f32[64,1,768]{2,1,0:T(1,128)} %reshape.135), calls=%async_computation | async-start | bytes 393216 | tf_op jit(solution)/shard_map/all_to_all | solution.py:12
  84.7 0.8 convolution_bitcast_fusion
  85.5 16.3 %all-to-all-done = f32[64,1,768]{2,1,0:T(1,128)S(1)} async-done(((f32[64,1,768]{2,1,0:T(1,128)}), f32[64,1,768]{2,1,0:T(1,128)S(1)}, u32[]{:S(2)}, u32[]{:S(2)}) %all-to-all-start) | async-done | bytes 196640 | tf_op jit(solution)/shard_map/all_to_all | solution.py:12
  101.8 0.5 broadcast.152
  102.3 1.1 reduce
  103.4 2.2 %reshape.136 = f32[64,2,6,4,16]{4,3,2,1,0:T(4,128)} reshape(f32[64,768]{1,0:T(8,128)S(1)} %reduce) | data formatting | bytes 393216
  105.7 3.1 %copy.257 = f32[64,4,2,6,16]{4,3,2,1,0:T(8,128)} copy(f32[64,4,2,6,16]{4,1,3,2,0:T(4,128)} %bitcast.378) | data formatting | bytes 393216 | tf_op jit(solution)/shard_map/all_to_all | solution.py:12
  108.8 2.4 %reshape_reshape.3 = f32[256,192]{1,0:T(8,128)S(1)} reshape(f32[64,4,2,6,16]{4,3,2,1,0:T(8,128)} %copy.257) | data formatting | bytes 393216 | tf_op jit(solution)/shard_map/reshape;reshape | solution.py:66
  111.1 2.9 %fusion.5 = f32[12,256,192]{1,2,0:T(8,128)S(1)} fusion(s32[256,12]{0,1:T(8,128)S(1)} %copy-done.7, f32[256,192]{1,0:T(8,128)S(1)} %reshape_reshape.3), kind=kOutput, calls=%fused_computation.140 | convolution fusion | flops 906756096 | bytes 2568192 | tf_op jit(solution)/shard_map/ilc,cs->lis/dot_general | solution.py:72
  114.1 0.5 subtract_reduce_fusion
  114.6 1.0 copy.259
  115.6 2.1 %reshape.137 = f32[64,1,768]{2,1,0:T(1,128)S(1)} reshape(f32[256,6,2,16]{3,2,1,0:T(2,128)S(1)} %bitcast.379) | data formatting | bytes 393216
  117.8 27.8 %all_to_all.23 = f32[64,1,768]{2,1,0:T(1,128)S(1)} all-to-all(f32[64,1,768]{2,1,0:T(1,128)S(1)} %reshape.137), channel_id=1, replica_groups=mesh['clus'=64,'samp'=8] {'clus'}, dimensions={0} | all-to-all | bytes 393216 | tf_op jit(solution)/shard_map/all_to_all | solution.py:79
  145.5 1.1 reduce.1
  146.6 2.1 %reshape.138 = f32[256,6,2,16]{3,2,1,0:T(2,128)S(1)} reshape(f32[64,768]{1,0:T(8,128)S(1)} %reduce.1) | data formatting | bytes 393216
  149.1 0.8 all_to_all.20
  150.3 0.2 add_bitcast_fusion
  150.7 2.8 %fusion.1 = f32[32,2,6,512]{3,0,2,1:T(8,128)S(1)} fusion(f32[32,1,6,1024]{3,0,2,1:T(8,128)S(1)} %get-tuple-element.17, f32[32,1,6,1024]{3,0,2,1:T(8,128)S(1)} %get-tuple-element.16, f32[1024]{0:T(1024)S(1)} %bitcast.405, s32[1024]{0:T(1024)S(1)} %bitcast.393, f32[1024]{0:T(1024)S(1)} %bitcast.407, s32[1024]{0:T(1024)S(1)} %bitcast.395, ...), kind=kOutput, calls=%fused_computation.2 | convolution fusion | flops 1217265664 | bytes 2408448 | tf_op jit(solution)/shard_map/cqan,pn->cqap/dot_general | solution.py:83
  153.6 3.8 %multiply_add_fusion.2 = f32[32,2,1,512]{3,0,2,1:T(8,128)S(1)} fusion(f32[32,2,6,512]{3,0,2,1:T(8,128)S(1)} %fusion.1, f32[]{:T(128)} %bitcast.52, f32[]{:T(128)} %bitcast.43, f32[]{:T(128)} %bitcast.34, f32[]{:T(128)} %bitcast.25, f32[]{:T(128)} %bitcast.16, f32[]{:T(128)} %bitcast.7), kind=kLoop, calls=%fused_computation.233 | loop fusion | flops 360448 | bytes 917528 | tf_op jit(solution)/shard_map/add | solution.py:88
  157.4 3.7 %multiply_add_fusion.1 = f32[32,2,1,512]{3,0,2,1:T(8,128)S(1)} fusion(f32[32,2,6,512]{3,0,2,1:T(8,128)S(1)} %fusion.1, f32[]{:T(128)} %bitcast.53, f32[]{:T(128)} %bitcast.44, f32[]{:T(128)} %bitcast.35, f32[]{:T(128)} %bitcast.26, f32[]{:T(128)} %bitcast.17, f32[]{:T(128)} %bitcast.8), kind=kLoop, calls=%fused_computation.232 | loop fusion | flops 360448 | bytes 917528 | tf_op jit(solution)/shard_map/add | solution.py:88
  161.0 3.8 %multiply_add_fusion = f32[32,2,1,512]{3,0,2,1:T(8,128)S(1)} fusion(f32[32,2,6,512]{3,0,2,1:T(8,128)S(1)} %fusion.1, f32[]{:T(128)} %bitcast.54, f32[]{:T(128)} %bitcast.45, f32[]{:T(128)} %bitcast.36, f32[]{:T(128)} %bitcast.27, f32[]{:T(128)} %bitcast.18, f32[]{:T(128)} %bitcast.9), kind=kLoop, calls=%fused_computation.231 | loop fusion | flops 360448 | bytes 917528 | tf_op jit(solution)/shard_map/add | solution.py:88
  164.9 4.0 %multiply_add_fusion.8 = f32[32,2,1,512]{3,0,2,1:T(8,128)S(1)} fusion(f32[32,2,6,512]{3,0,2,1:T(8,128)S(1)} %fusion.1, f32[]{:T(128)} %bitcast.49, f32[]{:T(128)} %bitcast.40, f32[]{:T(128)} %bitcast.31, f32[]{:T(128)} %bitcast.22, f32[]{:T(128)} %bitcast.13, f32[]{:T(128)} %bitcast.4), kind=kLoop, calls=%fused_computation.239 | loop fusion | flops 360448 | bytes 917528 | tf_op jit(solution)/shard_map/add | solution.py:88
  168.8 3.9 %multiply_add_fusion.5 = f32[32,2,1,512]{3,0,2,1:T(8,128)S(1)} fusion(f32[32,2,6,512]{3,0,2,1:T(8,128)S(1)} %fusion.1, f32[]{:T(128)} %bitcast.46, f32[]{:T(128)} %bitcast.37, f32[]{:T(128)} %bitcast.28, f32[]{:T(128)} %bitcast.19, f32[]{:T(128)} %bitcast.10, f32[]{:T(128)} %bitcast.1), kind=kLoop, calls=%fused_computation.236 | loop fusion | flops 360448 | bytes 917528 | tf_op jit(solution)/shard_map/add | solution.py:88
  172.7 3.8 %multiply_add_fusion.4 = f32[32,2,1,512]{3,0,2,1:T(8,128)S(1)} fusion(f32[32,2,6,512]{3,0,2,1:T(8,128)S(1)} %fusion.1, f32[]{:T(128)} %bitcast.47, f32[]{:T(128)} %bitcast.38, f32[]{:T(128)} %bitcast.29, f32[]{:T(128)} %bitcast.20, f32[]{:T(128)} %bitcast.11, f32[]{:T(128)} %bitcast.2), kind=kLoop, calls=%fused_computation.235 | loop fusion | flops 360448 | bytes 917528 | tf_op jit(solution)/shard_map/add | solution.py:88
  176.6 3.8 %multiply_add_fusion.3 = f32[32,2,1,512]{3,0,2,1:T(8,128)S(1)} fusion(f32[32,2,6,512]{3,0,2,1:T(8,128)S(1)} %fusion.1, f32[]{:T(128)} %bitcast.48, f32[]{:T(128)} %bitcast.39, f32[]{:T(128)} %bitcast.30, f32[]{:T(128)} %bitcast.21, f32[]{:T(128)} %bitcast.12, f32[]{:T(128)} %bitcast.3), kind=kLoop, calls=%fused_computation.234 | loop fusion | flops 360448 | bytes 917528 | tf_op jit(solution)/shard_map/add | solution.py:88
  180.4 5.4 %collective-permute-start.2 = (f32[32,2,3,512]{3,0,2,1:T(8,128)S(1)}, f32[32,2,3,512]{3,0,2,1:T(8,128)S(1)}, u32[]{:S(2)}, u32[]{:S(2)}) collective-permute-start(f32[32,2,3,512]{3,0,2,1:T(8,128)S(1)} %pad_maximum_fusion), channel_id=1, source_target_pairs={{0,7},{1,0},{2,1},{3,2},{4,3},{5,4},{6,5},{7,6},{8,15},{9,8},{10,9... | collective-permute-start | bytes 1179656 | tf_op jit(solution)/shard_map/ppermute | solution.py:18
  185.9 4.3 %collective-permute-start.3 = (f32[32,2,3,512]{3,0,2,1:T(8,128)S(1)}, f32[32,2,3,512]{3,0,2,1:T(8,128)S(1)}, u32[]{:S(2)}, u32[]{:S(2)}) collective-permute-start(f32[32,2,3,512]{3,0,2,1:T(8,128)S(1)} %pad_maximum_fusion.1), channel_id=1, source_target_pairs={{0,1},{1,2},{2,3},{3,4},{4,5},{5,6},{6,7},{7,0},{8,9},{9,10},{10,1... | collective-permute-start | bytes 1179656 | tf_op jit(solution)/shard_map/ppermute | solution.py:18
  190.2 3.9 %multiply_add_fusion.7 = f32[32,2,1,512]{3,0,2,1:T(8,128)S(1)} fusion(f32[32,2,6,512]{3,0,2,1:T(8,128)S(1)} %fusion.1, f32[]{:T(128)} %bitcast.50, f32[]{:T(128)} %bitcast.41, f32[]{:T(128)} %bitcast.32, f32[]{:T(128)} %bitcast.23, f32[]{:T(128)} %bitcast.14, f32[]{:T(128)} %bitcast.5), kind=kLoop, calls=%fused_computation.238 | loop fusion | flops 360448 | bytes 917528 | tf_op jit(solution)/shard_map/add | solution.py:88
  194.0 3.8 %multiply_add_fusion.6 = f32[32,2,1,512]{3,0,2,1:T(8,128)S(1)} fusion(f32[32,2,6,512]{3,0,2,1:T(8,128)S(1)} %fusion.1, f32[]{:T(128)} %bitcast.51, f32[]{:T(128)} %bitcast.42, f32[]{:T(128)} %bitcast.33, f32[]{:T(128)} %bitcast.24, f32[]{:T(128)} %bitcast.15, f32[]{:T(128)} %bitcast.6), kind=kLoop, calls=%fused_computation.237 | loop fusion | flops 360448 | bytes 917528 | tf_op jit(solution)/shard_map/add | solution.py:88
  198.0 1.1 copy.264
  (126 shorter events, 6.3 us)
Async XLA Ops:
  1.7 20.6 %collective-permute-start.1 = (f32[32,2,3,512]{3,0,2,1:T(8,128)S(1)}, f32[32,2,3,512]{3,0,2,1:T(8,128)S(1)}, u32[]{:S(2)}, u32[]{:S(2)}) collective-permute-start(f32[32,2,3,512]{3,0,2,1:T(8,128)S(1)} %copy.252), channel_id=1, source_target_pairs={{0,7},{1,0},{2,1},{3,2},{4,3},{5,4},{6,5},{7,6},{8,15},{9,8},{10,9... | collective-permute-start | bytes 1179656 | tf_op jit(solution)/shard_map/ppermute | solution.py:18
  10.5 11.9 %collective-permute-start = (f32[32,2,3,512]{3,0,2,1:T(8,128)S(1)}, f32[32,2,3,512]{3,0,2,1:T(8,128)S(1)}, u32[]{:S(2)}, u32[]{:S(2)}) collective-permute-start(f32[32,2,3,512]{3,0,2,1:T(8,128)S(1)} %copy.252), channel_id=1, source_target_pairs={{0,1},{1,2},{2,3},{3,4},{4,5},{5,6},{6,7},{7,0},{8,9},{9,10},{10,1... | collective-permute-start | bytes 1179656 | tf_op jit(solution)/shard_map/ppermute | solution.py:18
  15.5 41.4 %copy-start.8 = (s32[1024,1]{0,1:T(1,128)}, s32[1024,1]{0,1:T(1,128)S(1)}, u32[]{:S(2)}) copy-start(s32[1024,1]{0,1:T(1,128)S(1)} %get-tuple-element.26) | copy-start | bytes 12292
  15.5 41.4 %copy-start.10 = (s32[1024,1]{0,1:T(1,128)}, s32[1024,1]{0,1:T(1,128)S(1)}, u32[]{:S(2)}) copy-start(s32[1024,1]{0,1:T(1,128)S(1)} %get-tuple-element.27) | copy-start | bytes 12292
  16.5 40.4 %copy-start.12 = (f32[1024,1]{0,1:T(1,128)}, f32[1024,1]{0,1:T(1,128)S(1)}, u32[]{:S(2)}) copy-start(f32[1024,1]{0,1:T(1,128)S(1)} %get-tuple-element.28) | copy-start | bytes 12292
  16.6 40.4 %copy-start.14 = (f32[1024,1]{0,1:T(1,128)}, f32[1024,1]{0,1:T(1,128)S(1)}, u32[]{:S(2)}) copy-start(f32[1024,1]{0,1:T(1,128)S(1)} %get-tuple-element.29) | copy-start | bytes 12292
  16.6 40.4 %copy-start.16 = (f32[1024,1]{0,1:T(1,128)}, f32[1024,1]{0,1:T(1,128)S(1)}, u32[]{:S(2)}) copy-start(f32[1024,1]{0,1:T(1,128)S(1)} %get-tuple-element.30) | copy-start | bytes 12292
  16.6 40.4 %copy-start.18 = (f32[1024,1]{0,1:T(1,128)}, f32[1024,1]{0,1:T(1,128)S(1)}, u32[]{:S(2)}) copy-start(f32[1024,1]{0,1:T(1,128)S(1)} %get-tuple-element.31) | copy-start | bytes 12292
  16.6 40.4 %copy-start.20 = (f32[1024,1]{0,1:T(1,128)}, f32[1024,1]{0,1:T(1,128)S(1)}, u32[]{:S(2)}) copy-start(f32[1024,1]{0,1:T(1,128)S(1)} %get-tuple-element.32) | copy-start | bytes 12292
  16.6 40.4 %copy-start.22 = (f32[1024,1]{0,1:T(1,128)}, f32[1024,1]{0,1:T(1,128)S(1)}, u32[]{:S(2)}) copy-start(f32[1024,1]{0,1:T(1,128)S(1)} %get-tuple-element.33) | copy-start | bytes 12292
  22.3 37.5 %copy-start = (f32[8,6,1024]{2,0,1:T(8,128)}, f32[8,6,1024]{2,0,1:T(8,128)S(1)}, u32[]{:S(2)}) copy-start(f32[8,6,1024]{2,0,1:T(8,128)S(1)} %get-tuple-element.20) | copy-start | bytes 589828
  22.3 37.5 %copy-start.2 = (f32[8,6,1024]{2,0,1:T(8,128)}, f32[8,6,1024]{2,0,1:T(8,128)S(1)}, u32[]{:S(2)}) copy-start(f32[8,6,1024]{2,0,1:T(8,128)S(1)} %get-tuple-element.21) | copy-start | bytes 589828
  65.5 19.1 %copy-start.5 = (f32[16,2,6,16]{3,1,2,0:T(2,128)S(1)}, f32[16,2,6,16]{3,1,2,0:T(2,128)}, u32[]{:S(2)}) copy-start(f32[16,2,6,16]{3,1,2,0:T(2,128)} %param.13) | copy-start | bytes 36868
  65.6 19.1 %copy-start.6 = (s32[256,12]{0,1:T(8,128)S(1)}, s32[256,12]{0,1:T(8,128)}, u32[]{:S(2)}) copy-start(s32[256,12]{0,1:T(8,128)} %param.15) | copy-start | bytes 36868
  67.7 34.1 %all-to-all-start = ((f32[64,1,768]{2,1,0:T(1,128)}), f32[64,1,768]{2,1,0:T(1,128)S(1)}, u32[]{:S(2)}, u32[]{:S(2)}) async-start(f32[64,1,768]{2,1,0:T(1,128)} %reshape.135), calls=%async_computation | async-start | bytes 393216 | tf_op jit(solution)/shard_map/all_to_all | solution.py:12
  108.8 2.4 %copy-start.7 = (s32[256,12]{0,1:T(8,128)S(1)}, s32[256,12]{0,1:T(8,128)}, u32[]{:S(2)}) copy-start(s32[256,12]{0,1:T(8,128)} %param.14) | copy-start | bytes 36868
  149.1 1.2 copy-start.1
  149.1 1.2 copy-start.3
  149.9 3.6 %copy-start.4 = (f32[4,2,6,1024]{3,1,2,0:T(2,128)}, f32[4,2,6,1024]{3,1,2,0:T(2,128)S(1)}, u32[]{:S(2)}) copy-start(f32[4,2,6,1024]{3,1,2,0:T(2,128)S(1)} %all_to_all.20) | copy-start | bytes 589828
  149.9 0.7 copy-start.9
  149.9 0.7 copy-start.11
  150.0 0.7 copy-start.13
  150.0 0.7 copy-start.15
  150.0 0.7 copy-start.17
  150.0 0.7 copy-start.19
  150.0 0.7 copy-start.21
  150.0 0.7 copy-start.23
  180.4 17.4 %collective-permute-start.2 = (f32[32,2,3,512]{3,0,2,1:T(8,128)S(1)}, f32[32,2,3,512]{3,0,2,1:T(8,128)S(1)}, u32[]{:S(2)}, u32[]{:S(2)}) collective-permute-start(f32[32,2,3,512]{3,0,2,1:T(8,128)S(1)} %pad_maximum_fusion), channel_id=1, source_target_pairs={{0,7},{1,0},{2,1},{3,2},{4,3},{5,4},{6,5},{7,6},{8,15},{9,8},{10,9... | collective-permute-start | bytes 1179656 | tf_op jit(solution)/shard_map/ppermute | solution.py:18
  185.9 12.0 %collective-permute-start.3 = (f32[32,2,3,512]{3,0,2,1:T(8,128)S(1)}, f32[32,2,3,512]{3,0,2,1:T(8,128)S(1)}, u32[]{:S(2)}, u32[]{:S(2)}) collective-permute-start(f32[32,2,3,512]{3,0,2,1:T(8,128)S(1)} %pad_maximum_fusion.1), channel_id=1, source_target_pairs={{0,1},{1,2},{2,3},{3,4},{4,5},{5,6},{6,7},{7,0},{8,9},{9,10},{10,1... | collective-permute-start | bytes 1179656 | tf_op jit(solution)/shard_map/ppermute | solution.py:18
